TPU v7x, 128 devices: a whole 4x4x4 slice. The times are simulated.
128 devices in a mesh: row: 8 (over z, core), col: 16 (over y, x).
Axes of the slice: x: 4, y: 4, z: 4, core: 2. Of those that a mesh axis runs over, the one named last changes fastest.
Arguments:
- panel_first: bfloat16 [128, 256, 1024], P(('row', 'col')), may hold values from -3 to 3
- panel_second: bfloat16 [128, 256, 1024], P(('row', 'col')), may hold values from -4 to 4
- diag_first: bfloat16 [1024, 1024], P('col'), as said below
- bridge: bfloat16 [1024, 1024], P('col'), may hold values from -0.024902344 to 0.024902344
- diag_second: bfloat16 [1024, 1024], P('col'), as said below
- trailing: float32 [128, 24, 256, 256], P(('row', 'col')), may hold values from -6 to 6
- trail_pairs: int32 [128, 2, 24], P(('row', 'col')), may hold values from 0 to 15, as said below
- live_count: int32 [128], P(('row', 'col')), may hold values from 1 to 24, as said below
Outputs:
- lower_first: bfloat16 [128, 256, 1024], P(('row', 'col'))
- lower_second: bfloat16 [128, 256, 1024], P(('row', 'col'))
- trailing_out: float32 [128, 24, 256, 256], P(('row', 'col'))
Inputs may be any that keep to these rules, and one draw needn't show every extreme that they name: `trail_pairs`: on each device the listed pairs are distinct; the first entry of a pair is below 16 and the second below 8. `live_count`: some device has all 24 slots live in every draw. `diag_first`: symmetric and positive definite, with diagonal entries between 0.75 and 2.3. `diag_second`: symmetric and positive definite, with diagonal entries between 3.4 and 7.5.
All inputs are finite; a program needn't handle non-finite values.
Results may differ from a plain program's by a relative error of at most 0.001.
Values may be sent and summed in bfloat16 or wider, within the bound.
No kernel may reach another device: no remote copies, remote signals or barrier semaphores. Data moves between devices by JAX's collectives and lax.ppermute only.
A program may use at most 192 MiB of HBM per device.

v0:
```python
import jax
import jax.numpy as jnp
from jax import lax
from jax.sharding import PartitionSpec as P


def right_solve(lower_factor, block_rows):
    return jax.scipy.linalg.solve_triangular(lower_factor, block_rows.T, lower=True).T


def tile_product(left_tile, right_tile):
    return lax.dot_general(
        left_tile, right_tile, (((1,), (1,)), ((), ())), preferred_element_type=jnp.float32
    )


def apply_owned(trailing, row_tiles, col_tiles, pair_list, first_slot, stop_slot):

    def step_index(slot_index, carried):
        update = tile_product(
            row_tiles[pair_list[0, slot_index]], col_tiles[pair_list[1, slot_index]]
        )
        current = lax.dynamic_index_in_dim(carried, slot_index, 0, keepdims=False)
        return lax.dynamic_update_index_in_dim(carried, current - update, slot_index, 0)

    return lax.fori_loop(first_slot, stop_slot, step_index, trailing)


def update_tiles(trailing, row_tiles, col_tiles, pair_list, live_slots):
    return apply_owned(trailing, row_tiles, col_tiles, pair_list, 0, live_slots)


def per_device(
    panel_first, panel_second, diag_first, bridge, diag_second, trailing, trail_pairs, live_count
):
    highest = lax.Precision.HIGHEST
    whole_first, whole_bridge, whole_second = (
        lax.all_gather(diag_first, "col", axis=0, tiled=True),
        lax.all_gather(bridge, "col", axis=0, tiled=True),
        lax.all_gather(diag_second, "col", axis=0, tiled=True),
    )
    factor_first = jnp.linalg.cholesky(whole_first.astype(jnp.float32))
    coupling = right_solve(factor_first, whole_bridge.astype(jnp.float32))
    shifted = whole_second.astype(jnp.float32) - jnp.dot(
        coupling, coupling.T, precision=highest, preferred_element_type=jnp.float32
    )
    factor_second = jnp.linalg.cholesky(shifted)
    lower_first = right_solve(factor_first, panel_first[0].astype(jnp.float32)).astype(jnp.bfloat16)
    pair_list = trail_pairs[0]
    live_slots = live_count[0]
    owned = trailing[0]
    first_rows = lax.all_gather(lower_first[None], "col", axis=0, tiled=True)
    first_cols = lax.all_gather(lower_first[None], "row", axis=0, tiled=True)
    owned = update_tiles(owned, first_rows, first_cols, pair_list, live_slots)
    reduced = panel_second[0].astype(jnp.float32) - jnp.dot(
        lower_first.astype(jnp.float32),
        coupling.T,
        precision=highest,
        preferred_element_type=jnp.float32,
    )
    lower_second = right_solve(factor_second, reduced).astype(jnp.bfloat16)
    second_rows = lax.all_gather(lower_second[None], "col", axis=0, tiled=True)
    second_cols = lax.all_gather(lower_second[None], "row", axis=0, tiled=True)
    owned = update_tiles(owned, second_rows, second_cols, pair_list, live_slots)
    return (lower_first[None], lower_second[None], owned[None])


def solution(mesh):
    return jax.shard_map(
        per_device,
        mesh=mesh,
        in_specs=(
            P(("row", "col"), None, None),
            P(("row", "col"), None, None),
            P("col", None),
            P("col", None),
            P("col", None),
            P(("row", "col"), None, None, None),
            P(("row", "col"), None, None),
            P(("row", "col")),
        ),
        out_specs=(
            P(("row", "col"), None, None),
            P(("row", "col"), None, None),
            P(("row", "col"), None, None, None),
        ),
        check_vma=False,
    )
```

profile of v0, /device:TPU:73, one launch (start us, length us, event | category | flops | bytes accessed | tf_op | source)
XLA Modules:
  0.0 1385.7 jit_solution(17734967316498863521)
XLA Ops:
  15.1 42.9 %all-gather.12.cloned.1.call-done = bf16[1024,1024]{1,0:T(8,128)(2,1)} async-done(((bf16[64,1024]{1,0:T(8,128)(2,1)}), bf16[1024,1024]{1,0:T(8,128)(2,1)}) %all-gather.12.cloned.1.call-update) | async-done | bytes 2097168 | tf_op jit(solution)/shard_map/all_gather | solution.py:38
  68.7 11.7 cholesky.619
  96.7 11.7 cholesky.638
  109.1 10.1 custom-call.61
  122.6 11.7 cholesky.659
  149.0 11.9 cholesky.678
  175.5 11.7 cholesky.697
  201.9 11.7 cholesky.716
  227.8 11.7 cholesky.735
  240.8 10.2 custom-call.66
  253.6 11.7 cholesky.752
  277.2 23.1 %while.27 = (s32[]{:T(128)}, f32[1024,1024]{1,0:T(8,128)}, s32[8,2]{0,1:T(2,128)S(1)}, f32[8,128,128]{2,1,0:T(8,128)S(1)}, s32[]{:T(128)}) while((s32[]{:T(128)}, f32[1024,1024]{1,0:T(8,128)}, s32[8,2]{0,1:T(2,128)S(1)}, f32[8,128,128]{2,1,0:T(8,128)S(1)}, s32[]{:T(128)}) %tuple.178), condition=%wide.while_cond, body=%wide.while_body.sunk | while | flops 2 | bytes 131181 | solution.py:8
  300.3 78.8 %custom-call.67 = f32[8,128,128]{1,2,0:T(8,128)S(1)} custom-call(f32[8,128,128]{2,1,0:T(8,128)S(1)} %get-tuple-element.95), custom_call_target="InvertDiagBlocksLowerTriangular" | custom-call | tf_op jit(solution)/shard_map/jit(_solve_triangular)/triangular_solve | solution.py:8
  427.6 17.8 %convert_subtract_fusion = f32[1024,1024]{0,1:T(8,128)} fusion(bf16[1024,1024]{0,1:T(8,128)(2,1)S(1)} %copy.24, f32[1024,1024]{1,0:T(8,128)} %convolution_dynamic-update-slice_fusion), kind=kOutput, calls=%fused_computation.33 | convolution fusion | flops 12886999040 | bytes 10485760 | tf_op jit(solution)/shard_map/dot_general | solution.py:44
  457.5 11.7 cholesky.767
  485.5 11.9 cholesky.786
  512.6 11.7 cholesky.807
  538.9 11.9 cholesky.826
  565.4 11.7 cholesky.845
  578.4 10.2 custom-call.72
  591.9 11.7 cholesky.864
  617.7 11.9 cholesky.883
  643.3 11.7 cholesky.900
  666.5 23.1 %while.28 = (s32[]{:T(128)}, f32[1024,1024]{1,0:T(8,128)}, s32[8,2]{0,1:T(2,128)S(1)}, f32[8,128,128]{2,1,0:T(8,128)S(1)}, s32[]{:T(128)}) while((s32[]{:T(128)}, f32[1024,1024]{1,0:T(8,128)}, s32[8,2]{0,1:T(2,128)S(1)}, f32[8,128,128]{2,1,0:T(8,128)S(1)}, s32[]{:T(128)}) %tuple.211), condition=%wide.while_cond.clone, body=%wide.while_body.clone.sunk | while | flops 2 | bytes 131181 | solution.py:8
  689.6 79.4 %custom-call.75 = f32[8,128,128]{1,2,0:T(8,128)} custom-call(f32[8,128,128]{2,1,0:T(8,128)S(1)} %get-tuple-element.96), custom_call_target="InvertDiagBlocksLowerTriangular" | custom-call | tf_op jit(solution)/shard_map/jit(_solve_triangular)/triangular_solve | solution.py:8
  812.6 32.1 %all-gather.24.cloned.1.call-done = bf16[2048,1024]{0,1:T(8,128)(2,1)} async-done(((bf16[256,1024]{0,1:T(8,128)(2,1)}), bf16[2048,1024]{0,1:T(8,128)(2,1)}) %all-gather.24.cloned.1.call-update) | async-done | bytes 4194320 | tf_op jit(solution)/shard_map/all_gather | solution.py:63
  851.1 31.7 %all-gather.20.cloned.1.call-done = bf16[2048,1024]{0,1:T(8,128)(2,1)} async-done(((bf16[256,1024]{0,1:T(8,128)(2,1)}), bf16[2048,1024]{0,1:T(8,128)(2,1)}) %all-gather.20.cloned.1.call-update) | async-done | bytes 4194320 | tf_op jit(solution)/shard_map/all_gather | solution.py:53
  889.1 71.9 %all-gather.18.cloned.1.call-done = bf16[4096,1024]{0,1:T(8,128)(2,1)} async-done(((bf16[256,1024]{0,1:T(8,128)(2,1)}), bf16[4096,1024]{0,1:T(8,128)(2,1)}) %all-gather.18.cloned.1.call-update) | async-done | bytes 8388624 | tf_op jit(solution)/shard_map/all_gather | solution.py:52
  961.0 12.0 copy.34
  973.0 189.5 %while.25 = (s32[]{:T(128)}, f32[24,256,256]{2,1,0:T(8,128)}, s32[]{:T(128)}, s32[2,24]{1,0:T(2,128)S(1)}, bf16[16,256,1024]{2,1,0:T(8,128)(2,1)}, /*index=5*/bf...) while((s32[]{:T(128)}, f32[24,256,256]{2,1,0:T(8,128)}, ...), condition=%wide.region_17.20_spmd, body=%wide.region_16.19_spmd.sunk | while | flops 134283280 | bytes 2097399 | solution.py:26
  1162.6 12.0 copy.36
  1174.6 203.8 %while.26 = (s32[]{:T(128)}, f32[24,256,256]{2,1,0:T(8,128)}, s32[]{:T(128)}, s32[2,24]{1,0:T(2,128)S(1)}, bf16[16,256,1024]{2,1,0:T(8,128)(2,1)}, /*index=5*/bf...) while((s32[]{:T(128)}, f32[24,256,256]{2,1,0:T(8,128)}, ...), condition=%wide.region_19.22_spmd, body=%wide.region_18.21_spmd.sunk | while | flops 134283280 | bytes 2097399 | solution.py:26
  (384 shorter events, 554.7 us)
Async XLA Ops:
  7.2 7.8 copy-start.8
  7.2 50.8 %all-gather.12.cloned.1.call-start = ((), (), s32[]{:S(2)}) async-start(), calls=%async_computation | async-start | bytes 2228224 | tf_op jit(solution)/shard_map/all_gather | solution.py:38
  13.4 365.7 %all-gather.16.cloned.1.call-start = ((), (), s32[]{:S(2)}) async-start(), calls=%async_computation.2 | async-start | bytes 2228224 | tf_op jit(solution)/shard_map/all_gather | solution.py:39
  14.1 410.6 %all-gather.14.cloned.1.call-start = ((), (), s32[]{:S(2)}) async-start(), calls=%async_computation.1 | async-start | bytes 2228224 | tf_op jit(solution)/shard_map/all_gather | solution.py:40
  14.9 829.8 %all-gather.24.cloned.1.call-start = ((), (), s32[]{:S(2)}) async-start(), calls=%async_computation.6 | async-start | bytes 4718592 | tf_op jit(solution)/shard_map/all_gather | solution.py:63
  66.8 1.9 copy-start.1
  379.1 44.2 %copy-start.6 = (f32[8,128,128]{1,2,0:T(8,128)}, f32[8,128,128]{1,2,0:T(8,128)S(1)}, u32[]{:S(2)}) copy-start(f32[8,128,128]{1,2,0:T(8,128)S(1)} %custom-call.67) | copy-start | bytes 1572868
  379.1 2.5 copy-start.5
  455.6 2.0 copy-start
  661.5 107.5 %copy-start.7 = (f32[8,128,128]{1,2,0:T(8,128)S(1)}, f32[8,128,128]{1,2,0:T(8,128)}, u32[]{:S(2)}) copy-start(f32[8,128,128]{1,2,0:T(8,128)} %copy-done.6) | copy-start | bytes 1572868
  774.5 10.9 copy-start.9
  782.4 7.7 copy-start.10
  785.4 6.5 copy-start.2
  798.4 13.1 copy-start.3
  806.8 0.8 copy-start.4
  807.6 75.2 %all-gather.20.cloned.1.call-start = ((), (), s32[]{:S(2)}) async-start(), calls=%async_computation.4 | async-start | bytes 4718592 | tf_op jit(solution)/shard_map/all_gather | solution.py:53
  808.2 152.8 %all-gather.18.cloned.1.call-start = ((), (), s32[]{:S(2)}) async-start(), calls=%async_computation.3 | async-start | bytes 8912896 | tf_op jit(solution)/shard_map/all_gather | solution.py:52
  808.8 353.8 %all-gather.22.cloned.1.call-start = ((), (), s32[]{:S(2)}) async-start(), calls=%async_computation.5 | async-start | bytes 8912896 | tf_op jit(solution)/shard_map/all_gather | solution.py:62
  889.1 83.9 %copy-start.11 = (s32[1,2,24]{2,1,0:T(2,128)S(1)}, s32[1,2,24]{2,1,0:T(2,128)}, u32[]{:S(2)}) copy-start(s32[1,2,24]{2,1,0:T(2,128)} %param.21) | copy-start | bytes 580
Sparse Core Ops, SparseCore 0:
  13.5 44.4 all-gather.11
  60.1 44.5 all-gather.15
  106.9 44.3 all-gather.13
  807.7 36.9 all-gather.23
  846.2 36.5 all-gather.19
  884.7 76.2 all-gather.17
  963.1 76.4 all-gather.21
where the time goes:
time: 1410 us; the launch traced here: 1390 us
  other arithmetic  521 us (37%)
  matrix products  255 us (18%)
  loops' own time  208 us (15%)
  local copies, waits for them, and re-layouts  193 us (14%)
  waiting for transfers between devices  182 us (13%)
  between operations  25.7 us (2%)
    another operation x2, loops' own time, apply_owned(): return lax.fori_loop(first_slot, stop_slot, step_index, trailing)  208 us
    another operation x31, other arithmetic, per_device(): factor_second = jnp.linalg.cholesky(shifted)  173 us
    another operation x30, other arithmetic, per_device(): factor_first = jnp.linalg.cholesky(whole_first.astype(jnp.float32))  172 us
    another operation x5, other arithmetic, right_solve(): jax.scipy.linalg.solve_triangular(lower_factor, block_rows.T, lower=True)  168 us
    dot_general x48, matrix products, tile_product(): lax.dot_general(left_tile, right_tile, (((1,), (1,)), ((), ())), preferre...  108 us
    another operation x45, matrix products, right_solve(): jax.scipy.linalg.solve_triangular(lower_factor, block_rows.T, lower=True)  77.9 us
    all_gather x1, waiting for transfers between devices, per_device(): first_rows = lax.all_gather(lower_first[None], 'col', axis=0, tiled=True)  71.9 us
    dynamic_slice x48, local copies, waits for them, and re-layouts, step_index(): current = lax.dynamic_index_in_dim(carried, slot_index, 0, keepdims=False)  46.8 us
  transfers between devices with their start and end apart: 7, of which 4 were waited for; matrix products, arithmetic and copies ran while one was open for 35% of the time, Pallas kernels for 0%

commit v1 on v0

v1 whole, which is shorter than its diff:
```python
import jax
import jax.numpy as jnp
from jax import lax
from jax.experimental import pallas as pl
from jax.experimental.pallas import tpu as pltpu
from jax.sharding import PartitionSpec as P

F32, BF16 = jnp.float32, jnp.bfloat16
N, NB, Q = 1024, 128, 8


def split(x):
    hi = x.astype(BF16)
    return hi, (x - hi.astype(F32)).astype(BF16)


def dot(a, b, dims):
    return lax.dot_general(a, b, (dims, ((), ())), preferred_element_type=F32)


def diag_inverse(tiles):
    count = len(tiles)
    shape = (Q, NB)
    sub = lax.broadcasted_iota(jnp.int32, shape, 0)
    lane = lax.broadcasted_iota(jnp.int32, shape, 1)
    wide = lambda v: jnp.broadcast_to(v, shape)
    tiles = list(tiles)
    out = []
    for s in range(count):
        c0 = Q * s
        blk = tiles[s]
        cols = [wide(blk[:, c0 + m : c0 + m + 1]) for m in range(Q)]
        e = {(i, m): wide(cols[m][i : i + 1, :]) for m in range(Q) for i in range(m, Q)}
        r, l, v = [], {}, {}
        for m in range(Q):
            rm = lax.rsqrt(e[m, m])
            r.append(rm)
            for i in range(m + 1, Q):
                l[i, m] = e[i, m] * rm
            for j in range(m + 1, Q):
                for i in range(j, Q):
                    e[i, j] = e[i, j] - l[i, m] * l[j, m]
        for m in range(Q):
            v[m, m] = r[m]
            for i in range(m + 1, Q):
                acc = l[i, m] * v[m, m]
                for k in range(m + 1, i):
                    acc = acc + l[i, k] * v[k, m]
                v[i, m] = -(r[i] * acc)
        inside = (lane >= c0) & (lane < c0 + Q)
        tb = jnp.where(inside, jnp.where(lane - c0 == sub, 1.0, 0.0), blk)

        def combine(coef, src):
            total = None
            for k in range(Q):
                col = jnp.zeros(shape, F32)
                for i in range(Q):
                    got = coef(i, k)
                    if got is not None:
                        col = jnp.where(sub == i, got, col)
                term = col * wide(src[k : k + 1, :])
                total = term if total is None else total + term
            return total

        w = combine(lambda i, k: v[i, k] if i >= k else None, tb)
        out.append(jnp.where(lane < c0 + Q, w, 0.0))
        if s + 1 < count:
            z = combine(lambda i, k: v[k, i] if i <= k else None, w)
            zr = [wide(z[m : m + 1, :]) for m in range(Q)]
            for t in range(s + 1, count):
                row = tiles[t]
                total = None
                for m in range(Q):
                    term = wide(row[:, c0 + m : c0 + m + 1]) * zr[m]
                    total = term if total is None else total + term
                tiles[t] = jnp.where(inside, 0.0, row) - total
    return out


def factor(load_row, rh, rl, tri, start=None):
    blocks = N // NB
    lane = lax.broadcasted_iota(jnp.int32, (NB, N), 1)
    K0 = ((0,), (0,))
    KM = ((1,), (0,))

    def step(k, carry):
        k0 = pl.multiple_of(k * NB, NB)
        tri[...] = jnp.where(lane >= k0, load_row(k0), 0.0)
        for kk in range(1, blocks):

            @pl.when(k == kk)
            def _():
                h = kk * NB
                ah, al = rh[0:h, h : h + NB], rl[0:h, h : h + NB]
                bh, bl = rh[0:h, :], rl[0:h, :]
                tri[...] -= dot(ah, bh, K0) + dot(ah, bl, K0) + dot(al, bh, K0)
                rh[0:h, h : h + NB] = jnp.zeros((h, NB), BF16)
                rl[0:h, h : h + NB] = jnp.zeros((h, NB), BF16)

        d = tri[:, pl.ds(k0, NB)]
        tiles = diag_inverse([d[Q * i : Q * i + Q, :] for i in range(NB // Q)])
        w = jnp.concatenate(tiles, axis=0)
        tri[:, pl.ds(k0, NB)] = jnp.eye(NB, dtype=F32)
        wh, wl = split(w)
        xh, xl = split(tri[...])
        row = dot(wh, xh, KM) + dot(wh, xl, KM) + dot(wl, xh, KM)
        oh, ol = split(row)
        rh[pl.ds(k0, NB), :] = oh
        rl[pl.ds(k0, NB), :] = ol
        return carry

    lax.fori_loop(0, blocks, step, 0)


def first_kernel(g_ref, oh, ol, tri):
    def load(k0):
        i = k0 // 64
        return jnp.concatenate(
            [g_ref[i, 0:64, :], g_ref[i + 1, 0:64, :]], axis=0
        ).astype(F32)

    factor(load, oh, ol, tri)


def second_kernel(g_ref, w1h, w1l, oh, ol, gh, gl, ch, cl, shifted, tri):
    KT = ((1,), (1,))
    KM = ((1,), (0,))
    half = 256
    for i in range(N // half):
        for j in range(N // half):
            s, t, kk = slice(i * half, i * half + half), slice(j * half, j * half + half), half * (j + 1)
            b = jnp.concatenate([g_ref[4 * i + q, 64:128, 0:kk] for q in range(4)], axis=0)
            hi, lo = split(dot(b, w1h[t, 0:kk], KT) + dot(b, w1l[t, 0:kk], KT))
            ch[s, t] = hi
            cl[s, t] = lo
    for i in range(N // half):
        for j in range(i, N // half):
            s, t = slice(i * half, i * half + half), slice(j * half, j * half + half)
            d = jnp.concatenate([g_ref[4 * i + q, 128:192, t] for q in range(4)], axis=0)
            prod = dot(ch[s, :], ch[t, :], KT) + dot(ch[s, :], cl[t, :], KT) + dot(cl[s, :], ch[t, :], KT)
            shifted[s, t] = d.astype(F32) - prod
    factor(lambda k0: shifted[pl.ds(k0, NB), :], oh, ol, tri)
    for i in range(N // half):
        for j in range(N // half):
            s, t, kk = slice(i * half, i * half + half), slice(j * half, j * half + half), half * (i + 1)
            hi, lo = split(
                dot(oh[s, 0:kk], ch[0:kk, t], KM)
                + dot(oh[s, 0:kk], cl[0:kk, t], KM)
                + dot(ol[s, 0:kk], ch[0:kk, t], KM)
            )
            gh[s, t] = hi
            gl[s, t] = lo


VM = pl.BlockSpec(memory_space=pltpu.VMEM)
LIMIT = 60 * 1024 * 1024


def first_stage(g):
    return pl.pallas_call(
        first_kernel,
        out_shape=[jax.ShapeDtypeStruct((N, N), BF16)] * 2,
        in_specs=[VM],
        out_specs=[VM] * 2,
        scratch_shapes=[pltpu.VMEM((NB, N), F32)],
        compiler_params=pltpu.CompilerParams(vmem_limit_bytes=LIMIT),
        cost_estimate=pl.CostEstimate(flops=10**10, bytes_accessed=10**7, transcendentals=0),
        name="first_stage",
    )(g)


def second_stage(g, w1h, w1l):
    return pl.pallas_call(
        second_kernel,
        out_shape=[jax.ShapeDtypeStruct((N, N), BF16)] * 4,
        in_specs=[VM] * 3,
        out_specs=[VM] * 4,
        scratch_shapes=[pltpu.VMEM((N, N), BF16)] * 2
        + [pltpu.VMEM((N, N), F32)]
        + [pltpu.VMEM((NB, N), F32)],
        compiler_params=pltpu.CompilerParams(vmem_limit_bytes=LIMIT),
        cost_estimate=pl.CostEstimate(flops=2 * 10**10, bytes_accessed=10**7, transcendentals=0),
        name="second_stage",
    )(g, w1h, w1l)


PER, GROUP = 2, 4


def final_kernel(
    pairs, live, need_col, need_row, own,
    col_p, row_p, w1h, w1l, w2h, w2l, gh, gl, tin,
    own_first, own_second, tout, lcol, lrow,
):
    KT = ((1,), (1,))
    step = pl.program_id(0)
    half = 256
    ncol, nrow = lcol.shape[0] // PER, lrow.shape[0] // PER

    def solve(src, dst, base):
        p1 = jnp.concatenate([src[u, 0] for u in range(PER)], axis=0)
        for j in range(N // half):
            t, kk = slice(j * half, j * half + half), half * (j + 1)
            got = dot(p1[:, 0:kk], w1h[t, 0:kk], KT) + dot(p1[:, 0:kk], w1l[t, 0:kk], KT)
            got = got.astype(BF16)
            for u in range(PER):
                dst[base + u, :, t] = got[u * half : u * half + half, :]
        p2 = jnp.concatenate([src[u, 1] for u in range(PER)], axis=0)
        l1 = jnp.concatenate([dst[base + u, :, 0:N] for u in range(PER)], axis=0)
        for j in range(N // half):
            t, kk = slice(j * half, j * half + half), half * (j + 1)
            got = dot(p2[:, 0:kk], w2h[t, 0:kk], KT) + dot(p2[:, 0:kk], w2l[t, 0:kk], KT)
            got = got - (dot(l1, gh[t, :], KT) + dot(l1, gl[t, :], KT))
            got = got.astype(BF16)
            for u in range(PER):
                dst[base + u, :, N + j * half : N + j * half + half] = got[u * half : u * half + half, :]

    @pl.when(step < ncol)
    def _():
        @pl.when(need_col[jnp.minimum(step, ncol - 1)] > 0)
        def _():
            solve(col_p, lcol, PER * step)

    @pl.when((step >= ncol) & (step < ncol + nrow))
    def _():
        at = jnp.clip(step - ncol, 0, nrow - 1)

        @pl.when(need_row[at] > 0)
        def _():
            solve(row_p, lrow, PER * at)

    @pl.when(step == ncol + nrow - 1)
    def _():
        own_first[0] = lrow[own[0], :, 0:N]
        own_second[0] = lrow[own[0], :, N : 2 * N]

    @pl.when(step >= ncol + nrow)
    def _():
        base = (step - ncol - nrow) * GROUP
        for u in range(GROUP):
            slot = base + u

            @pl.when(slot < live[0])
            def _():
                a, b = pairs[slot], pairs[24 + slot]
                tout[0, u] = tin[0, u] - dot(lrow[a], lcol[b], KT)

            @pl.when(slot >= live[0])
            def _():
                tout[0, u] = tin[0, u]


def final_stage(pairs, live, need_col, need_row, own, col_p, row_p, weights, trailing):
    ncol, nrow = col_p.shape[0], row_p.shape[0]
    slots = trailing.shape[1]
    cs, rs = ncol // PER, nrow // PER
    ks = slots // GROUP
    tiles = lambda lo, cnt: (lambda s, *_: (jnp.clip(s - lo, 0, cnt - 1), 0, 0, 0))
    tmap = lambda s, *_: (0, jnp.clip(s - cs - rs, 0, ks - 1), 0, 0)
    once = pl.BlockSpec((N, N), lambda s, *_: (0, 0), pipeline_mode=pl.Buffered(1))
    own_spec = pl.BlockSpec((1, 256, N), lambda s, *_: (0, 0, 0))
    return pl.pallas_call(
        final_kernel,
        out_shape=[
            jax.ShapeDtypeStruct((1, 256, N), BF16),
            jax.ShapeDtypeStruct((1, 256, N), BF16),
            jax.ShapeDtypeStruct(trailing.shape, F32),
        ],
        grid_spec=pltpu.PrefetchScalarGridSpec(
            num_scalar_prefetch=5,
            grid=(cs + rs + ks,),
            in_specs=[
                pl.BlockSpec((PER, 2, 256, N), tiles(0, cs)),
                pl.BlockSpec((PER, 2, 256, N), tiles(cs, rs)),
            ]
            + [once] * 6
            + [pl.BlockSpec((1, GROUP, 256, 256), tmap)],
            out_specs=[own_spec, own_spec, pl.BlockSpec((1, GROUP, 256, 256), tmap)],
            scratch_shapes=[pltpu.VMEM((ncol, 256, 2 * N), BF16), pltpu.VMEM((nrow, 256, 2 * N), BF16)],
        ),
        compiler_params=pltpu.CompilerParams(
            vmem_limit_bytes=LIMIT, dimension_semantics=("arbitrary",)
        ),
        cost_estimate=pl.CostEstimate(flops=6 * 10**10, bytes_accessed=4 * 10**7, transcendentals=0),
        name="final_stage",
    )(pairs, live, need_col, need_row, own, col_p, row_p, *weights, trailing)


def per_device(
    panel_first, panel_second, diag_first, bridge, diag_second, trailing, trail_pairs, live_count
):
    blocks = lax.all_gather(
        jnp.concatenate([diag_first, bridge, diag_second], axis=0), "col", axis=0
    )
    both = jnp.stack([panel_first[0], panel_second[0]], axis=0)
    row_p = lax.all_gather(both, "col", axis=0)
    col_p = lax.all_gather(both, "row", axis=0)
    own = lax.axis_index("col").astype(jnp.int32)
    pairs = trail_pairs[0]
    active = jnp.arange(pairs.shape[1], dtype=jnp.int32) < live_count[0]
    group_r = jnp.arange(row_p.shape[0] // PER, dtype=jnp.int32)
    group_c = jnp.arange(col_p.shape[0] // PER, dtype=jnp.int32)
    need_row = jnp.any((pairs[0][None] // PER == group_r[:, None]) & active[None], axis=1) | (group_r == own // PER)
    need_col = jnp.any((pairs[1][None] // PER == group_c[:, None]) & active[None], axis=1)
    w1h, w1l = first_stage(blocks)
    w2h, w2l, gh, gl = second_stage(blocks, w1h, w1l)
    return final_stage(
        pairs.reshape(-1), live_count, need_col.astype(jnp.int32), need_row.astype(jnp.int32), own[None],
        col_p, row_p, (w1h, w1l, w2h, w2l, gh, gl), trailing,
    )


def solution(mesh):
    return jax.shard_map(
        per_device,
        mesh=mesh,
        in_specs=(
            P(("row", "col"), None, None),
            P(("row", "col"), None, None),
            P("col", None),
            P("col", None),
            P("col", None),
            P(("row", "col"), None, None, None),
            P(("row", "col"), None, None),
            P(("row", "col")),
        ),
        out_specs=(
            P(("row", "col"), None, None),
            P(("row", "col"), None, None),
            P(("row", "col"), None, None, None),
        ),
        check_vma=False,
    )
```

time: 1410 us -> 341 us (0.24)
  the two profiles are of different devices: /device:TPU:73 before, /device:TPU:30 now
where the time goes in v1:
time: 341 us; the launch traced here: 335 us
  Pallas kernels  209 us (61%)
  waiting for transfers between devices  105 us (31%)
  between operations  14.5 us (4%)
    pallas_call x1, Pallas kernels, final_stage(): pl.pallas_call(final_kernel, out_shape=[jax.ShapeDtypeStruct((1, 256, N),...  90.3 us
    pallas_call x1, Pallas kernels, second_stage(): pl.pallas_call(second_kernel, out_shape=[jax.ShapeDtypeStruct((N, N), BF1...  65.9 us
    all_gather x1, waiting for transfers between devices, per_device(): lax.all_gather(jnp.concatenate([diag_first, bridge, diag_second], axis=0)...  57.4 us
    pallas_call x1, Pallas kernels, first_stage(): pl.pallas_call(first_kernel, out_shape=[jax.ShapeDtypeStruct((N, N), BF16...  53.1 us
    all_gather x1, waiting for transfers between devices, per_device(): row_p = lax.all_gather(both, 'col', axis=0)  46.8 us
  transfers between devices with their start and end apart: 3, of which 2 were waited for; matrix products, arithmetic and copies ran while one was open for 1% of the time, Pallas kernels for 36%

profile of v1, /device:TPU:30, one launch (start us, length us, event | category | flops | bytes accessed | tf_op | source)
XLA Modules:
  0.0 334.7 jit_solution(14743251083590014640)
XLA Ops:
  7.2 0.0 copy-start.1
  7.2 0.0 all-gather.11.cloned.1.call-start
  7.2 1.9 pad_maximum_fusion
  9.1 0.0 all-gather.11.cloned.1.call-update
  9.1 0.0 copy-start.2
  9.1 0.0 all-gather.7.cloned.1.call-start
  9.2 1.1 constant_dynamic-update-slice_fusion.1
  10.2 0.0 copy-done.1
  10.3 0.0 copy-start
  10.3 1.0 copy-done
  11.3 0.0 all-gather.7.cloned.1.call-update
  11.3 0.0 all-gather.9.cloned.1.call-start
  11.3 0.7 all-gather.9.cloned.1.call-update
  12.7 0.0 copy-done.2
  12.7 0.6 reshape_squeeze.3.pairs
  13.3 0.1 fusion.3
  13.4 0.5 convert_element_type.6.need_col
  14.0 0.1 fusion.1
  14.1 0.6 or_convert_fusion.need_row
  14.6 57.4 %all-gather.11.cloned.1.call-done = bf16[3072,1024]{1,0:T(8,128)(2,1)} async-done(((bf16[192,1024]{1,0:T(8,128)(2,1)}), bf16[3072,1024]{1,0:T(8,128)(2,1)}) %all-gather.11.cloned.1.call-update) | async-done | bytes 6291472 | tf_op jit(solution)/shard_map/all_gather | solution.py:292
  72.0 53.1 %first_stage.1 = (bf16[1024,1024]{1,0:T(8,128)(2,1)}, bf16[1024,1024]{1,0:T(8,128)(2,1)}) custom-call(bf16[16,192,1024]{2,1,0:T(8,128)(2,1)} %bitcast.24), custom_call_target="tpu_custom_call" | custom-call | flops 10000000000 | bytes 10000000 | tf_op jit(solution)/shard_map/first_stage/pallas_call | solution.py:160
  125.1 65.9 %second_stage.1 = (bf16[1024,1024]{1,0:T(8,128)(2,1)}, bf16[1024,1024]{1,0:T(8,128)(2,1)}, bf16[1024,1024]{1,0:T(8,128)(2,1)}, bf16[1024,1024]{1,0:T(8,128)(2,1)}) custom-call(bf16[16,192,1024]{2,1,0:T(8,128)(2,1)} %bitcast.25, bf16[1024,1024]{1,0:T(8,128)(2,1)} %get-tuple-element.9.w1h, bf16[1024,1024]{1,0:T(8,128)(2,1)} %get-tuple-element.10.w1l), custom_call_target="tpu_custom_call" | custom-call | flops 20000000000 | bytes 10000000 | tf_op jit(solution)/shard_map/second_stage/pallas_call | solution.py:173
  191.0 0.0 all-gather.7.cloned.1.call-done
  191.0 46.8 %all-gather.9.cloned.1.call-done = bf16[32,256,1024]{2,1,0:T(8,128)(2,1)} async-done(((bf16[2,256,1024]{2,1,0:T(8,128)(2,1)}), bf16[32,256,1024]{2,1,0:T(8,128)(2,1)}) %all-gather.9.cloned.1.call-update) | async-done | bytes 16777232 | tf_op jit(solution)/shard_map/all_gather | solution.py:296
  237.8 90.3 %final_stage.1 = (bf16[1,256,1024]{2,1,0:T(8,128)(2,1)}, bf16[1,256,1024]{2,1,0:T(8,128)(2,1)}, f32[1,24,256,256]{3,2,1,0:T(8,128)}) custom-call(s32[48]{0:T(128)} %reshape_squeeze.3.pairs, s32[1]{0:T(128)} %copy.12.live, s32[4]{0:T(128)} %convert_element_type.6.need_col, s32[8]{0:T(128)} %or_convert_fusion.need_row, s32[1]{0:T(128)} %bitcast.3.own, ...), custom_call_target="tpu_custom_call" | custom-call | flops 60000002048 | bytes 40000000 | tf_op jit(solution)/shard_map/final_stage/pallas_call | solution.py:262
  (3 shorter events, 0.1 us)
Async XLA Ops:
  7.2 3.1 copy-start.1
  7.2 64.8 %all-gather.11.cloned.1.call-start = ((), (), s32[]{:S(2)}) async-start(), calls=%async_computation.2 | async-start | bytes 6684672 | tf_op jit(solution)/shard_map/all_gather | solution.py:292
  9.1 3.6 %copy-start.2 = (s32[1,2,24]{2,1,0:T(2,128)S(1)}, s32[1,2,24]{2,1,0:T(2,128)}, u32[]{:S(2)}) copy-start(s32[1,2,24]{2,1,0:T(2,128)} %param.14) | copy-start | bytes 580
  9.1 181.9 %all-gather.7.cloned.1.call-start = ((), (), s32[]{:S(2)}) async-start(), calls=%async_computation | async-start | bytes 9437184 | tf_op jit(solution)/shard_map/all_gather | solution.py:297
  10.3 1.0 copy-start
  11.3 226.5 %all-gather.9.cloned.1.call-start = ((), (), s32[]{:S(2)}) async-start(), calls=%async_computation.1 | async-start | bytes 17825792 | tf_op jit(solution)/shard_map/all_gather | solution.py:296
Sparse Core Ops, SparseCore 0:
  10.7 61.2 all-gather.10
  74.3 51.4 all-gather.6
  128.5 109.1 all-gather.8
